TPU v7x, 128 devices: a whole 4x4x4 slice. The times are simulated.
128 devices in a mesh: rows: 32 (over x, z, core), rel: 4 (over y).
Axes of the slice: x: 4, y: 4, z: 4, core: 2. Of those that a mesh axis runs over, the one named last changes fastest.
Arguments:
- features: bfloat16 [16384, 256], P('rows'), may hold values from -6 to 6
- bases: bfloat16 [8, 256, 256], replicated, may hold values from -0.125 to 0.125
- root: bfloat16 [256, 256], replicated, may hold values from -0.375 to 0.375
- coeffs: float32 [800, 8], P('rel'), may hold values from -4 to 4
- tiles: bfloat16 [32, 4, 64, 128, 128], P('rows', 'rel'), as said below
- tile_dst: int32 [32, 4, 64], P('rows', 'rel'), may hold values from 0 to 3
- tile_src: int32 [32, 4, 64], P('rows', 'rel'), may hold values from 0 to 63
- tile_rel: int32 [32, 4, 64], P('rows', 'rel'), may hold values from 0 to 199
- tile_live: int32 [32, 4], P('rows', 'rel'), may hold values from 16 to 64, as said below
- send_list: int32 [32, 4, 32, 2], P('rows', 'rel'), may hold values from 0 to 3
- cotangent: bfloat16 [16384, 256], P('rows'), may hold values from -6 to 6
Outputs:
- output: bfloat16 [16384, 256], P('rows')
- feature_grad: float32 [16384, 256], P('rows')
- basis_grad: float32 [8, 256, 256], replicated
- root_grad: float32 [256, 256], replicated
Inputs may be any that keep to these rules, and one draw needn't show every extreme that they name: `tile_live`: at least one device uses all 64 tile slots. `tiles`: entries are zero or positive, at most 12 / sqrt(2048).
All inputs are finite; a program needn't handle non-finite values.
Results may differ from a plain program's by a relative error of at most 0.0029.
Values may be sent and summed in bfloat16 or wider, within the bound.
A program may use at most 128 MiB of HBM per device.

v0:
```python
import math

import jax
import jax.numpy as jnp
from jax import lax
from jax.sharding import PartitionSpec as P


def on_device(
    features,
    bases,
    root,
    coeffs,
    tiles,
    tile_dst,
    tile_src,
    tile_rel,
    tile_live,
    send_list,
    cotangent,
):
    highest = lax.Precision.HIGHEST
    contract_first = (((0,), (0,)), ((), ()))
    feat_width = features.shape[1]
    size_block = tiles.shape[-1]
    blocks = features.reshape(-1, size_block, feat_width)
    local_blocks = blocks.shape[0]
    num_bases = bases.shape[0]
    slots_peer = send_list.shape[-1]
    row_devices = lax.axis_size("rows")
    total_slots = row_devices * slots_peer
    count_tiles = tiles.shape[2]
    adjacency = tiles[0, 0]
    dst_ids = tile_dst[0, 0]
    src_ids = tile_src[0, 0]
    rel_ids = tile_rel[0, 0]
    live_count = tile_live[0, 0]
    send_rows = send_list[0, 0]
    outgoing = blocks[send_rows]
    incoming = lax.all_to_all(outgoing, "rows", split_axis=0, concat_axis=0, tiled=True)
    received = incoming.reshape(total_slots, size_block, feat_width)
    step_tiles = math.gcd(count_tiles, 64)
    steps_live = (live_count + step_tiles - 1) // step_tiles

    def tile_weights(first_tile):
        position = first_tile + jnp.arange(step_tiles)
        in_use = (position < live_count).astype(jnp.float32)
        rel_hot = (rel_ids[:, None] == jnp.arange(coeffs.shape[0])[None, :]).astype(jnp.float32)
        coef_rows = jnp.dot(rel_hot, coeffs, precision=highest)
        dst_hot = (dst_ids[:, None] == jnp.arange(local_blocks)[None, :]).astype(
            jnp.float32
        ) * in_use[:, None]
        return (dst_hot[:, :, None] * coef_rows[:, None, :]).reshape(
            step_tiles, local_blocks * num_bases
        )

    def forward_step(block_index, running):
        first_tile = block_index * step_tiles
        sources = received[src_ids]
        messages = jnp.einsum(
            "tij,tjf->tif", adjacency, sources, preferred_element_type=jnp.float32
        )
        weights = tile_weights(first_tile)
        return running + lax.dot_general(
            weights, messages.reshape(step_tiles, -1), contract_first, precision=highest
        )

    zero_total = jnp.zeros((local_blocks * num_bases, size_block * feat_width), jnp.float32)
    partial_value = lax.fori_loop(0, steps_live, forward_step, zero_total)
    partial_value = partial_value.reshape(local_blocks, num_bases, size_block, feat_width)
    basis_f32 = bases.astype(jnp.float32)
    cot_blocks = cotangent.reshape(local_blocks, size_block, feat_width)
    cot_f32 = cot_blocks.astype(jnp.float32)
    root_term = jnp.dot(features, root, preferred_element_type=jnp.float32)
    root_local = lax.dot_general(
        features, cotangent, contract_first, preferred_element_type=jnp.float32
    )
    aggregate = lax.psum(partial_value, "rel")
    projected = jnp.einsum("lbnf,bfg->lng", aggregate, basis_f32, precision=highest)
    basis_local = jnp.einsum("lbnf,lng->bfg", aggregate, cot_f32, precision=highest)
    basis_grad, root_grad = lax.psum((basis_local, root_local), "rows")
    output = (projected.reshape(-1, feat_width) + root_term).astype(jnp.bfloat16)
    agg_grad = jnp.einsum("lng,bfg->lbnf", cot_blocks, bases, preferred_element_type=jnp.float32)
    agg_grad = agg_grad.reshape(local_blocks * num_bases, size_block * feat_width)

    def backward_step(block_index, running):
        first_tile = block_index * step_tiles
        weights = tile_weights(first_tile)
        spread = jnp.dot(weights, agg_grad, precision=highest).astype(jnp.bfloat16)
        spread = spread.reshape(step_tiles, size_block, feat_width)
        backward_term = jnp.einsum(
            "tij,tif->tjf", adjacency, spread, preferred_element_type=jnp.float32
        )
        slot_hot = (src_ids[:, None] == jnp.arange(total_slots)[None, :]).astype(jnp.float32)
        return running + lax.dot_general(
            slot_hot, backward_term.reshape(step_tiles, -1), contract_first, precision=highest
        )

    slot_zero = jnp.zeros((total_slots, size_block * feat_width), jnp.float32)
    slot_grads = lax.fori_loop(0, steps_live, backward_step, slot_zero)
    returned = lax.all_to_all(
        slot_grads.reshape(row_devices, slots_peer, size_block * feat_width),
        "rows",
        split_axis=0,
        concat_axis=0,
        tiled=True,
    )
    block_hot = (send_rows.reshape(-1)[None, :] == jnp.arange(local_blocks)[:, None]).astype(
        jnp.float32
    )
    own_grads = jnp.dot(block_hot, returned.reshape(total_slots, -1), precision=highest)
    summed = lax.psum(own_grads, "rel")
    root_back = lax.dot_general(
        cotangent, root, (((1,), (1,)), ((), ())), preferred_element_type=jnp.float32
    )
    feature_grad = summed.reshape(-1, feat_width) + root_back
    return (output, feature_grad, basis_grad, root_grad)


def solution(mesh):
    return jax.shard_map(
        on_device,
        mesh=mesh,
        in_specs=(
            P("rows", None),
            P(),
            P(),
            P("rel", None),
            P("rows", "rel", None, None, None),
            P("rows", "rel", None),
            P("rows", "rel", None),
            P("rows", "rel", None),
            P("rows", "rel"),
            P("rows", "rel", None, None),
            P("rows", None),
        ),
        out_specs=(P("rows", None), P("rows", None), P(), P()),
        check_vma=False,
    )
```

profile of v0, /device:TPU:1, one launch (start us, length us, event | category | flops | bytes accessed | tf_op | source)
XLA Modules:
  0.0 457.6 jit_solution(15787599625584917114)
XLA Ops:
  8.2 3.7 gather_fusion
  11.9 9.6 %all-to-all-start = ((bf16[32,2,128,256]{3,2,1,0:T(8,128)(2,1)}), bf16[32,2,128,256]{3,2,1,0:T(8,128)(2,1)}, u32[]{:S(2)}, u32[]{:S(2)}) async-start(bf16[32,2,128,256]{3,2,1,0:T(8,128)(2,1)} %bitcast.130), calls=%async_computation | async-start | bytes 8388608 | tf_op jit(solution)/shard_map/all_to_all | solution.py:40
  22.2 2.7 convolution_bitcast_fusion.1
  24.9 5.5 %copy.36 = f32[4,8,128,256]{3,1,2,0:T(8,128)} copy(f32[4,8,128,256]{2,3,0,1:T(8,128)} %convolution_bitcast_fusion.1) | data formatting | bytes 8388608
  30.6 3.9 broadcast_in_dim.5
  34.5 38.4 %while.25 = (s32[]{:T(128)}, f32[64,32768]{1,0:T(8,128)}, s32[]{:T(128)}, s32[1,1,64]{2,1,0:T(1,128)S(1)}, s32[1,1,64]{2,1,0:T(1,128)S(1)}, /*index=5*/s32[]{:T(...) while((s32[]{:T(128)}, f32[64,32768]{1,0:T(8,128)}, ...), condition=%wide.region_4.5_spmd, body=%wide.region_3.4_spmd.sunk | while | flops 2956991232 | bytes 73405568 | solution.py:100
  35.4 8.6 %convolution_convert_fusion.2 = bf16[64,32768]{1,0:T(8,128)(2,1)S(1)} fusion(f32[32,32768]{1,0:T(8,128)} %get-tuple-element.440, f32[64,8]{0,1:T(8,128)S(1)} %get-tuple-element.439, f32[64,4]{0,1:T(4,128)S(1)} %fusion.64), kind=kOutput, calls=%fused_computation.11.clone.1 | convolution fusion | flops 807405568 | bytes 8391680 | tf_op jit(solution)/shard_map/while/body/dot_general | solution.py:89
  44.0 1.1 copy.45
  45.1 4.5 convolution_bitcast_fusion.4
  49.6 9.2 %copy.46 = f32[8,8,128,256]{3,1,2,0:T(8,128)} copy(f32[8,8,128,256]{2,3,1,0:T(8,128)} %bitcast.122) | data formatting | bytes 16777216 | tf_op jit(solution)/shard_map/while
  58.8 14.1 %convolution_add_fusion.7 = f32[64,32768]{1,0:T(8,128)} fusion(f32[64,32768]{1,0:T(8,128)} %get-tuple-element.423, f32[64,32768]{1,0:T(8,128)} %bitcast.121, s32[64]{0:T(128)S(1)} %bitcast.136), kind=kOutput, calls=%fused_computation.10.clone.1 | convolution fusion | flops 1612713984 | bytes 25166080 | tf_op jit(solution)/shard_map/while/body/dot_general | solution.py:95
  72.9 10.6 %reshape.243 = f32[32,2,32768]{2,1,0:T(2,128)} reshape(f32[64,32768]{1,0:T(8,128)} %get-tuple-element.236) | data formatting | bytes 16777216 | tf_op jit(solution)/shard_map/reshape | solution.py:102
  83.6 7.6 %all-to-all-start.1 = ((f32[32,2,32768]{2,1,0:T(2,128)}), f32[32,2,32768]{2,1,0:T(2,128)}, u32[]{:S(2)}, u32[]{:S(2)}) async-start(f32[32,2,32768]{2,1,0:T(2,128)} %reshape.243), calls=%async_computation.1 | async-start | bytes 16777216 | tf_op jit(solution)/shard_map/all_to_all | solution.py:101
  91.4 4.9 %gather_fusion.1 = bf16[64,128,256]{2,1,0:T(8,128)(2,1)} fusion(bf16[64,128,256]{2,1,0:T(8,128)(2,1)} %bitcast.12, s32[1024]{0:T(1024)S(1)} %pad_clamp_fusion), kind=kCustom, calls=%fused_computation.1 | custom fusion | bytes 8388864 | tf_op jit(solution)/shard_map/while/body/gather | solution.py:59
  96.3 2.3 broadcast_in_dim.4
  98.6 16.0 %while.24 = (s32[]{:T(128)}, f32[32,32768]{1,0:T(8,128)}, s32[]{:T(128)}, s32[1,1,64]{2,1,0:T(1,128)S(1)}, s32[]{:T(128)}, /*index=5*/f32[64,8]{0,1:T(8,128)S(1)...) while((s32[]{:T(128)}, f32[32,32768]{1,0:T(8,128)}, s32[]{:T(128)}, ...), condition=%wide.region_1.2_spmd, body=%wide.region_0.1_spmd.sunk | while | flops 1343228672 | bytes 48239480 | solution.py:69
  99.3 3.4 fusion.57
  102.7 4.7 %copy.44 = f32[8,8,128,256]{3,1,2,0:T(8,128)S(1)} copy(f32[8,8,128,256]{3,2,1,0:T(8,128)S(1)} %bitcast.123) | data formatting | bytes 16777216 | tf_op jit(solution)/shard_map/while
  107.5 7.1 %convolution_add_fusion.6 = f32[32,32768]{1,0:T(8,128)} fusion(f32[32,32768]{1,0:T(8,128)} %get-tuple-element.392, f32[64,32768]{1,0:T(8,128)S(1)} %bitcast.120, f32[64,8]{0,1:T(8,128)S(1)} %get-tuple-element.406, f32[64,4]{0,1:T(4,128)S(1)} %fusion.58), kind=kOutput, calls=%fused_computation.2.clone.1 | convolution fusion | flops 806356992 | bytes 16780288 | tf_op jit(solution)/shard_map/while/body/dot_general | solution.py:64
  114.6 5.4 %copy.40 = f32[4,8,128,256]{3,2,1,0:T(8,128)} copy(f32[4,8,128,256]{3,1,2,0:T(8,128)} %bitcast.127) | data formatting | bytes 8388608
  120.0 78.3 %all-to-all-done.1 = f32[32,2,32768]{2,1,0:T(2,128)} async-done(((f32[32,2,32768]{2,1,0:T(2,128)}), f32[32,2,32768]{2,1,0:T(2,128)}, u32[]{:S(2)}, u32[]{:S(2)}) %all-to-all-start.1) | async-done | bytes 8388640 | tf_op jit(solution)/shard_map/all_to_all | solution.py:101
  198.3 10.9 %reshape.244 = f32[64,32768]{1,0:T(8,128)} reshape(f32[32,2,32768]{2,1,0:T(2,128)} %all-to-all-done.1) | data formatting | bytes 16777216 | tf_op jit(solution)/shard_map/reshape | solution.py:111
  209.3 6.2 %fusion.17 = f32[4,32768]{1,0:T(4,128)S(1)} fusion(f32[64,32768]{1,0:T(8,128)} %reshape.244, s32[64]{0:T(128)S(1)} %eq.116), kind=kOutput, calls=%fused_computation.39 | convolution fusion | flops 100663552 | bytes 8913152 | tf_op jit(solution)/shard_map/dot_general | solution.py:111
  215.5 1.2 reshape.245
  216.7 1.0 fusion.21
  217.7 114.5 %all-reduce.7.cloned.1.call-done = (f32[4,8,128,256]{3,2,1,0:T(8,128)}, f32[512,256]{1,0:T(8,128)}) async-done(((f32[4,8,128,256]{3,2,1,0:T(8,128)}, f32[512,256]{1,0:T(8,128)}), (f32[4,8,128,256]{3,2,1,0:T(8,128)}, f32[512,256]{1,0:T(8,128)})) %all-reduce.7.cloned.1.call-update) | async-done | bytes 4718608 | tf_op jit(solution)/shard_map/psum | solution.py:78
  332.1 6.9 %convolution_bitcast_fusion.2 = f32[8,256,256]{2,1,0:T(8,128)} fusion(f32[4,8,128,256]{3,2,1,0:T(8,128)} %get-tuple-element.273, bf16[4,128,256,1]{2,1,3,0:T(8,128)(2,1)S(1)} %bitcast.132), kind=kOutput, calls=%fused_computation.24 | convolution fusion | flops 3221225472 | bytes 6553600 | tf_op jit(solution)/shard_map/lbnf,lng->bfg/dot_general | solution.py:80
  339.1 4.3 fusion.13
  343.4 0.9 fusion.11
  344.3 1.1 convolution_add_fusion.2
  345.4 101.6 %all-reduce.5.cloned.1.call-done = (f32[8,256,256]{2,1,0:T(8,128)}, f32[256,256]{1,0:T(8,128)}) async-done(((f32[8,256,256]{2,1,0:T(8,128)}, f32[256,256]{1,0:T(8,128)}), (f32[8,256,256]{2,1,0:T(8,128)}, f32[256,256]{1,0:T(8,128)})) %all-reduce.5.cloned.1.call-update) | async-done | bytes 2359312 | tf_op jit(solution)/shard_map/psum | solution.py:81
  447.0 3.1 copy.65
  (45 shorter events, 3.6 us)
Async XLA Ops:
  7.2 15.0 %copy-start = (bf16[8,256,256]{2,1,0:T(8,128)(2,1)S(1)}, bf16[8,256,256]{2,1,0:T(8,128)(2,1)}, u32[]{:S(2)}) copy-start(bf16[8,256,256]{2,1,0:T(8,128)(2,1)} %param.16) | copy-start | bytes 3145732
  11.9 10.3 %copy-start.3 = (bf16[512,256]{1,0:T(8,128)(2,1)S(1)}, bf16[512,256]{1,0:T(8,128)(2,1)}, u32[]{:S(2)}) copy-start(bf16[512,256]{1,0:T(8,128)(2,1)} %param.25) | copy-start | bytes 786436
  11.9 71.7 %all-to-all-start = ((bf16[32,2,128,256]{3,2,1,0:T(8,128)(2,1)}), bf16[32,2,128,256]{3,2,1,0:T(8,128)(2,1)}, u32[]{:S(2)}, u32[]{:S(2)}) async-start(bf16[32,2,128,256]{3,2,1,0:T(8,128)(2,1)} %bitcast.130), calls=%async_computation | async-start | bytes 8388608 | tf_op jit(solution)/shard_map/all_to_all | solution.py:40
  24.9 5.5 %copy-start.11 = (f32[200,8]{0,1:T(8,128)S(1)}, f32[200,8]{0,1:T(8,128)}, u32[]{:S(2)}) copy-start(f32[200,8]{0,1:T(8,128)} %param.18) | copy-start | bytes 19204
  24.9 5.5 %copy-start.12 = (s32[1,1,64]{2,1,0:T(1,128)S(1)}, s32[1,1,64]{2,1,0:T(1,128)}, u32[]{:S(2)}) copy-start(s32[1,1,64]{2,1,0:T(1,128)} %param.22) | copy-start | bytes 772
  30.6 4.0 copy-start.1
  30.6 4.0 copy-start.8
  30.6 4.0 copy-start.9
  83.6 7.6 %copy-start.10 = (s32[1,1,32,2]{2,3,1,0:T(2,128)S(1)}, s32[1,1,32,2]{2,3,1,0:T(2,128)}, u32[]{:S(2)}) copy-start(s32[1,1,32,2]{2,3,1,0:T(2,128)} %param.24) | copy-start | bytes 772
  83.6 114.8 %all-to-all-start.1 = ((f32[32,2,32768]{2,1,0:T(2,128)}), f32[32,2,32768]{2,1,0:T(2,128)}, u32[]{:S(2)}, u32[]{:S(2)}) async-start(f32[32,2,32768]{2,1,0:T(2,128)} %reshape.243), calls=%async_computation.1 | async-start | bytes 16777216 | tf_op jit(solution)/shard_map/all_to_all | solution.py:101
  91.1 241.0 %all-reduce.7.cloned.1.call-start = ((), (), s32[]{:S(2)}) async-start(), calls=%async_computation.3 | async-start | bytes 9437184 | tf_op jit(solution)/shard_map/psum | solution.py:78
  215.4 1.2 copy-start.2
  215.5 1.3 copy-start.4
  216.6 230.3 %all-reduce.5.cloned.1.call-start = ((), (), s32[]{:S(2)}) async-start(), calls=%async_computation.2 | async-start | bytes 4718592 | tf_op jit(solution)/shard_map/psum | solution.py:81
  339.1 4.3 copy-start.6
  339.1 5.2 %copy-start.5 = (f32[512,256]{1,0:T(8,128)S(1)}, f32[512,256]{1,0:T(8,128)}, u32[]{:S(2)}) copy-start(f32[512,256]{1,0:T(8,128)} %get-tuple-element.274) | copy-start | bytes 1572868
  447.0 3.1 copy-start.7
Sparse Core Ops, SparseCore 0:
  216.8 115.3 all-reduce.6
  339.2 107.6 all-reduce.4
where the time goes:
time: 459 us; the launch traced here: 458 us
  waiting for transfers between devices  294 us (64%)
  local copies, waits for them, and re-layouts  67.8 us (15%)
  matrix products  60.9 us (13%)
  starting transfers between devices  17.3 us (4%)
  between operations  14.8 us (3%)
    psum x1, waiting for transfers between devices, on_device(): aggregate = lax.psum(partial_value, 'rel')  114 us
    psum x1, waiting for transfers between devices, on_device(): basis_grad, root_grad = lax.psum((basis_local, root_local), 'rows')  102 us
    all_to_all x1, waiting for transfers between devices, on_device(): lax.all_to_all(slot_grads.reshape(row_devices, slots_peer, size_block * f...  78.3 us
    while x3, local copies, waits for them, and re-layouts  15 us
    unnamed x31, local copies, waits for them, and re-layouts  14.9 us
    dot_general x1, matrix products, backward_step(): lax.dot_general(slot_hot, backward_term.reshape(step_tiles, -1), contract...  14.1 us
    reshape x1, local copies, waits for them, and re-layouts, on_device(): returned.reshape(total_slots, -1)  10.9 us
    reshape x1, local copies, waits for them, and re-layouts, on_device(): slot_grads.reshape(row_devices, slots_peer, size_block * feat_width)  10.6 us
  transfers between devices with their start and end apart: 4, of which 3 were waited for; matrix products, arithmetic and copies ran while one was open for 21% of the time, Pallas kernels for 0%

commit v1 on v0

--- a/solution.py
+++ b/solution.py
@@ -72,13 +72,18 @@
     cot_blocks = cotangent.reshape(local_blocks, size_block, feat_width)
     cot_f32 = cot_blocks.astype(jnp.float32)
     root_term = jnp.dot(features, root, preferred_element_type=jnp.float32)
+    rel_devices = lax.axis_size("rel")
+    part_rows = features.shape[0] // rel_devices
+    first_row = lax.axis_index("rel") * part_rows
+    feat_part = lax.dynamic_slice_in_dim(features, first_row, part_rows)
+    cot_part = lax.dynamic_slice_in_dim(cotangent, first_row, part_rows)
     root_local = lax.dot_general(
-        features, cotangent, contract_first, preferred_element_type=jnp.float32
+        feat_part, cot_part, contract_first, preferred_element_type=jnp.float32
     )
-    aggregate = lax.psum(partial_value, "rel")
-    projected = jnp.einsum("lbnf,bfg->lng", aggregate, basis_f32, precision=highest)
-    basis_local = jnp.einsum("lbnf,lng->bfg", aggregate, cot_f32, precision=highest)
-    basis_grad, root_grad = lax.psum((basis_local, root_local), "rows")
+    projected_part = jnp.einsum("lbnf,bfg->lng", partial_value, basis_f32, precision=highest)
+    basis_local = jnp.einsum("lbnf,lng->bfg", partial_value, cot_f32, precision=highest)
+    projected = lax.psum(projected_part, "rel")
+    basis_grad, root_grad = lax.psum((basis_local, root_local), ("rows", "rel"))
     output = (projected.reshape(-1, feat_width) + root_term).astype(jnp.bfloat16)
     agg_grad = jnp.einsum("lng,bfg->lbnf", cot_blocks, bases, preferred_element_type=jnp.float32)
     agg_grad = agg_grad.reshape(local_blocks * num_bases, size_block * feat_width)
@@ -109,6 +114,7 @@
         jnp.float32
     )
     own_grads = jnp.dot(block_hot, returned.reshape(total_slots, -1), precision=highest)
+    own_grads, projected = lax.optimization_barrier((own_grads, projected))
     summed = lax.psum(own_grads, "rel")
     root_back = lax.dot_general(
         cotangent, root, (((1,), (1,)), ((), ())), preferred_element_type=jnp.float32

time: 459 us -> 448 us (0.976)
  waiting for transfers between devices: 294 us -> 279 us
  matrix products: 60.9 us -> 66.1 us
    psum x2 -> x3, waiting for transfers between devices: 216 us -> 204 us  [the longest x1 158 us: on_device(): basis_grad, root_grad = lax.psum((basis_local, root_local), ('rows', 'rel'))]
    unnamed x31 -> x28, local copies, waits for them, and re-layouts: 14.9 us -> 9.45 us
    while x3 -> x7, local copies, waits for them, and re-layouts: 15 us -> 17 us
  transfers between devices with their start and end apart: 4 -> 5, of which waited for: 3 -> 3; matrix products, arithmetic and copies ran while one was open for 21% -> 27% of each run, Pallas kernels for 0% -> 0%
where the time goes in v1:
time: 448 us; the launch traced here: 444 us
  waiting for transfers between devices  279 us (62%)
  matrix products  66.1 us (15%)
  local copies, waits for them, and re-layouts  64.4 us (14%)
  starting transfers between devices  17.4 us (4%)
  between operations  14.8 us (3%)
    psum x1, waiting for transfers between devices, on_device(): basis_grad, root_grad = lax.psum((basis_local, root_local), ('rows', 'rel'))  158 us
    all_to_all x1, waiting for transfers between devices, on_device(): lax.all_to_all(slot_grads.reshape(row_devices, slots_peer, size_block * f...  75.4 us
    psum x1, waiting for transfers between devices, on_device(): summed = lax.psum(own_grads, 'rel')  45.5 us
    while x7, local copies, waits for them, and re-layouts  17 us
    dot_general x1, matrix products, backward_step(): lax.dot_general(slot_hot, backward_term.reshape(step_tiles, -1), contract...  14.1 us
    reshape x1, local copies, waits for them, and re-layouts, on_device(): returned.reshape(total_slots, -1)  10.9 us
    reshape x1, local copies, waits for them, and re-layouts, on_device(): slot_grads.reshape(row_devices, slots_peer, size_block * feat_width)  10.6 us
    all_to_all x1, starting transfers between devices, on_device(): lax.all_to_all(outgoing, 'rows', split_axis=0, concat_axis=0, tiled=True)  9.61 us
  transfers between devices with their start and end apart: 5, of which 3 were waited for; matrix products, arithmetic and copies ran while one was open for 27% of the time, Pallas kernels for 0%

profile of v1, /device:TPU:1, one launch (start us, length us, event | category | flops | bytes accessed | tf_op | source)
XLA Modules:
  0.0 444.5 jit_solution(7627320191184519020)
XLA Ops:
  8.2 3.7 gather_fusion
  11.9 9.6 %all-to-all-start = ((bf16[32,2,128,256]{3,2,1,0:T(8,128)(2,1)}), bf16[32,2,128,256]{3,2,1,0:T(8,128)(2,1)}, u32[]{:S(2)}, u32[]{:S(2)}) async-start(bf16[32,2,128,256]{3,2,1,0:T(8,128)(2,1)} %bitcast.121), calls=%async_computation | async-start | bytes 8388608 | tf_op jit(solution)/shard_map/all_to_all | solution.py:40
  22.2 2.7 convolution_bitcast_fusion.1
  24.8 5.5 %copy.36 = f32[4,8,128,256]{3,1,2,0:T(8,128)} copy(f32[4,8,128,256]{2,3,0,1:T(8,128)} %convolution_bitcast_fusion.1) | data formatting | bytes 8388608
  30.6 4.0 broadcast_in_dim.5
  34.5 40.2 %while.25 = (s32[]{:T(128)}, f32[64,32768]{1,0:T(8,128)}, s32[]{:T(128)}, s32[1,1,64]{2,1,0:T(1,128)S(1)}, s32[1,1,64]{2,1,0:T(1,128)S(1)}, /*index=5*/s32[]{:T(...) while((s32[]{:T(128)}, f32[64,32768]{1,0:T(8,128)}, ...), condition=%wide.region_4.5_spmd, body=%wide.region_3.4_spmd.sunk | while | flops 2956991232 | bytes 73405568 | solution.py:105
  35.7 8.6 %convolution_convert_fusion.2 = bf16[64,32768]{1,0:T(8,128)(2,1)S(1)} fusion(f32[32,32768]{1,0:T(8,128)} %get-tuple-element.440, f32[64,8]{0,1:T(8,128)S(1)} %get-tuple-element.439, f32[64,4]{0,1:T(4,128)S(1)} %fusion.72), kind=kOutput, calls=%fused_computation.11.clone.1 | convolution fusion | flops 807405568 | bytes 8391680 | tf_op jit(solution)/shard_map/while/body/dot_general | solution.py:94
  44.2 1.1 copy.51
  45.3 6.1 %convolution_bitcast_fusion.3 = f32[64,128,256]{1,2,0:T(8,128)} fusion(bf16[64,128,256]{2,1,0:T(8,128)(2,1)S(1)} %bitcast.115, bf16[64,128,128]{2,1,0:T(8,128)(2,1)} %get-tuple-element.441), kind=kOutput, calls=%fused_computation.12.clone.1 | convolution fusion | flops 536870912 | bytes 14680064 | tf_op jit(solution)/shard_map/while/body/tij,tif->tjf/dot_general | solution.py:96
  51.5 9.2 %copy.52 = f32[8,8,128,256]{3,1,2,0:T(8,128)} copy(f32[8,8,128,256]{2,3,1,0:T(8,128)} %bitcast.113) | data formatting | bytes 16777216 | tf_op jit(solution)/shard_map/while
  60.7 14.1 %convolution_add_fusion.7 = f32[64,32768]{1,0:T(8,128)} fusion(f32[64,32768]{1,0:T(8,128)} %get-tuple-element.423, f32[64,32768]{1,0:T(8,128)} %bitcast.112, s32[64]{0:T(128)S(1)} %bitcast.127), kind=kOutput, calls=%fused_computation.10.clone.1 | convolution fusion | flops 1612713984 | bytes 25166080 | tf_op jit(solution)/shard_map/while/body/dot_general | solution.py:100
  74.8 10.6 %reshape.243 = f32[32,2,32768]{2,1,0:T(2,128)} reshape(f32[64,32768]{1,0:T(8,128)} %get-tuple-element.237) | data formatting | bytes 16777216 | tf_op jit(solution)/shard_map/reshape | solution.py:107
  85.4 7.4 %all-to-all-start.1 = ((f32[32,2,32768]{2,1,0:T(2,128)}), f32[32,2,32768]{2,1,0:T(2,128)}, u32[]{:S(2)}, u32[]{:S(2)}) async-start(f32[32,2,32768]{2,1,0:T(2,128)} %reshape.243), calls=%async_computation.1 | async-start | bytes 16777216 | tf_op jit(solution)/shard_map/all_to_all | solution.py:106
  92.9 4.9 %gather_fusion.1 = bf16[64,128,256]{2,1,0:T(8,128)(2,1)} fusion(bf16[64,128,256]{2,1,0:T(8,128)(2,1)} %bitcast.12, s32[1024]{0:T(1024)S(1)} %pad_clamp_fusion), kind=kCustom, calls=%fused_computation.1 | custom fusion | bytes 8388864 | tf_op jit(solution)/shard_map/while/body/gather | solution.py:59
  97.9 2.3 broadcast_in_dim.4
  100.1 18.3 %while.24 = (s32[]{:T(128)}, f32[32,32768]{1,0:T(8,128)}, s32[]{:T(128)}, s32[1,1,64]{2,1,0:T(1,128)S(1)}, s32[]{:T(128)}, /*index=5*/f32[64,8]{0,1:T(8,128)S(1)...) while((s32[]{:T(128)}, f32[32,32768]{1,0:T(8,128)}, s32[]{:T(128)}, ...), condition=%wide.region_1.2_spmd, body=%wide.region_0.1_spmd.sunk | while | flops 1343228672 | bytes 81793968 | solution.py:69
  100.8 4.1 fusion.65
  104.9 4.7 %copy.50 = f32[8,8,128,256]{3,1,2,0:T(8,128)S(1)} copy(f32[8,8,128,256]{3,2,1,0:T(8,128)S(1)} %bitcast.114) | data formatting | bytes 16777216 | tf_op jit(solution)/shard_map/while
  109.6 6.6 %convolution_add_fusion.6 = f32[32,32768]{1,0:T(8,128)S(1)} fusion(f32[32,32768]{1,0:T(8,128)S(1)} %copy-done.1, f32[64,32768]{1,0:T(8,128)S(1)} %bitcast.111, f32[64,8]{0,1:T(8,128)S(1)} %get-tuple-element.406, f32[64,4]{0,1:T(4,128)S(1)} %fusion.66), kind=kOutput, calls=%fused_computation.2.clone.1 | convolution fusion | flops 806356992 | bytes 16780288 | tf_op jit(solution)/shard_map/while/body/dot_general | solution.py:64
  116.3 2.0 copy-done.2
  118.4 6.0 %fusion.18 = f32[4,128,256]{2,1,0:T(8,128)} fusion(f32[4,8,128,256]{3,1,2,0:T(8,128)} %bitcast.117, bf16[8,256,256]{2,1,0:T(8,128)(2,1)S(1)} %copy-done), kind=kOutput, calls=%fused_computation.28 | convolution fusion | flops 3221225472 | bytes 5767168 | tf_op jit(solution)/shard_map/lbnf,bfg->lng/dot_general | solution.py:83
  124.7 75.4 %all-to-all-done.1 = f32[32,2,32768]{2,1,0:T(2,128)} async-done(((f32[32,2,32768]{2,1,0:T(2,128)}), f32[32,2,32768]{2,1,0:T(2,128)}, u32[]{:S(2)}, u32[]{:S(2)}) %all-to-all-start.1) | async-done | bytes 8388640 | tf_op jit(solution)/shard_map/all_to_all | solution.py:106
  200.1 10.9 %reshape.244 = f32[64,32768]{1,0:T(8,128)} reshape(f32[32,2,32768]{2,1,0:T(2,128)} %all-to-all-done.1) | data formatting | bytes 16777216 | tf_op jit(solution)/shard_map/reshape | solution.py:116
  211.0 6.2 %fusion.29 = f32[4,32768]{1,0:T(4,128)S(1)} fusion(f32[64,32768]{1,0:T(8,128)} %reshape.244, s32[64]{0:T(128)S(1)} %eq.116), kind=kOutput, calls=%fused_computation.45 | convolution fusion | flops 100663552 | bytes 8913152 | tf_op jit(solution)/shard_map/dot_general | solution.py:116
  217.2 1.2 reshape.245
  218.7 0.9 fusion.24
  219.6 7.6 %fusion.15 = f32[8,256,256]{2,1,0:T(8,128)} fusion(bf16[4,128,256,1]{2,1,0,3:T(8,128)(2,1)S(1)} %bitcast.123, f32[4,8,128,256]{3,1,2,0:T(8,128)} %bitcast.118), kind=kOutput, calls=%fused_computation.27 | convolution fusion | flops 3221225472 | bytes 6553600 | tf_op jit(solution)/shard_map/lbnf,lng->bfg/dot_general | solution.py:84
  227.3 0.9 fusion.21
  228.2 45.5 %all-reduce.7.cloned.1.call-done = f32[512,256]{1,0:T(8,128)} async-done(((f32[512,256]{1,0:T(8,128)}), f32[512,256]{1,0:T(8,128)}) %all-reduce.7.cloned.1.call-update) | async-done | bytes 524304 | tf_op jit(solution)/shard_map/psum | solution.py:118
  273.7 2.1 convolution_add_fusion.2
  275.8 158.1 %all-reduce.9.cloned.1.call-done = (f32[8,256,256]{2,1,0:T(8,128)}, f32[256,256]{1,0:T(8,128)}) async-done(((f32[8,256,256]{2,1,0:T(8,128)}, f32[256,256]{1,0:T(8,128)}), (f32[8,256,256]{2,1,0:T(8,128)}, f32[256,256]{1,0:T(8,128)})) %all-reduce.9.cloned.1.call-update) | async-done | bytes 2359312 | tf_op jit(solution)/shard_map/psum | solution.py:86
  433.9 3.1 copy.70
  (49 shorter events, 3.8 us)
Async XLA Ops:
  7.2 15.0 %copy-start = (bf16[8,256,256]{2,1,0:T(8,128)(2,1)S(1)}, bf16[8,256,256]{2,1,0:T(8,128)(2,1)}, u32[]{:S(2)}) copy-start(bf16[8,256,256]{2,1,0:T(8,128)(2,1)} %param.16) | copy-start | bytes 3145732
  11.9 10.3 %copy-start.4 = (bf16[512,256]{1,0:T(8,128)(2,1)S(1)}, bf16[512,256]{1,0:T(8,128)(2,1)}, u32[]{:S(2)}) copy-start(bf16[512,256]{1,0:T(8,128)(2,1)} %param.25) | copy-start | bytes 786436
  11.9 73.5 %all-to-all-start = ((bf16[32,2,128,256]{3,2,1,0:T(8,128)(2,1)}), bf16[32,2,128,256]{3,2,1,0:T(8,128)(2,1)}, u32[]{:S(2)}, u32[]{:S(2)}) async-start(bf16[32,2,128,256]{3,2,1,0:T(8,128)(2,1)} %bitcast.121), calls=%async_computation | async-start | bytes 8388608 | tf_op jit(solution)/shard_map/all_to_all | solution.py:40
  24.8 5.5 %copy-start.12 = (f32[200,8]{0,1:T(8,128)S(1)}, f32[200,8]{0,1:T(8,128)}, u32[]{:S(2)}) copy-start(f32[200,8]{0,1:T(8,128)} %param.18) | copy-start | bytes 19204
  24.8 5.5 %copy-start.13 = (s32[1,1,64]{2,1,0:T(1,128)S(1)}, s32[1,1,64]{2,1,0:T(1,128)}, u32[]{:S(2)}) copy-start(s32[1,1,64]{2,1,0:T(1,128)} %param.22) | copy-start | bytes 772
  30.6 4.0 copy-start.9
  30.6 4.0 copy-start.10
  85.4 114.7 %all-to-all-start.1 = ((f32[32,2,32768]{2,1,0:T(2,128)}), f32[32,2,32768]{2,1,0:T(2,128)}, u32[]{:S(2)}, u32[]{:S(2)}) async-start(f32[32,2,32768]{2,1,0:T(2,128)} %reshape.243), calls=%async_computation.1 | async-start | bytes 16777216 | tf_op jit(solution)/shard_map/all_to_all | solution.py:106
  92.9 124.4 %all-reduce.5.cloned.1.call-start = ((), (), s32[]{:S(2)}) async-start(), calls=%async_computation.2 | async-start | bytes 1048576 | tf_op jit(solution)/shard_map/psum | solution.py:85
  104.9 4.8 %copy-start.1 = (f32[32,32768]{1,0:T(8,128)S(1)}, f32[32,32768]{1,0:T(8,128)}, u32[]{:S(2)}) copy-start(f32[32,32768]{1,0:T(8,128)} %get-tuple-element.392) | copy-start | bytes 12582916 | tf_op jit(solution)/shard_map/while
  116.3 2.0 copy-start.2
  118.4 6.1 %copy-start.11 = (s32[1,1,32,2]{2,3,1,0:T(2,128)S(1)}, s32[1,1,32,2]{2,3,1,0:T(2,128)}, u32[]{:S(2)}) copy-start(s32[1,1,32,2]{2,3,1,0:T(2,128)} %param.24) | copy-start | bytes 772
  124.4 149.3 %all-reduce.7.cloned.1.call-start = ((), (), s32[]{:S(2)}) async-start(), calls=%async_computation.3 | async-start | bytes 1048576 | tf_op jit(solution)/shard_map/psum | solution.py:118
  211.0 7.7 %copy-start.3 = (bf16[512,256]{1,0:T(8,128)(2,1)S(1)}, bf16[512,256]{1,0:T(8,128)(2,1)}, u32[]{:S(2)}) copy-start(bf16[512,256]{1,0:T(8,128)(2,1)} %param.15) | copy-start | bytes 786436
  211.0 7.7 %copy-start.5 = (bf16[512,256]{1,0:T(8,128)(2,1)S(1)}, bf16[512,256]{1,0:T(8,128)(2,1)}, u32[]{:S(2)}) copy-start(bf16[512,256]{1,0:T(8,128)(2,1)} %param.25) | copy-start | bytes 786436
  218.4 215.5 %all-reduce.9.cloned.1.call-start = ((), (), s32[]{:S(2)}) async-start(), calls=%async_computation.4 | async-start | bytes 4718592 | tf_op jit(solution)/shard_map/psum | solution.py:86
  219.6 7.7 %copy-start.6 = (f32[4,128,256]{2,1,0:T(8,128)S(1)}, f32[4,128,256]{2,1,0:T(8,128)}, u32[]{:S(2)}) copy-start(f32[4,128,256]{2,1,0:T(8,128)} %all-reduce.5.cloned.1.call-done) | copy-start | bytes 1572868
  219.6 7.7 %copy-start.7 = (bf16[256,256]{1,0:T(8,128)(2,1)S(1)}, bf16[256,256]{1,0:T(8,128)(2,1)}, u32[]{:S(2)}) copy-start(bf16[256,256]{1,0:T(8,128)(2,1)} %param.17) | copy-start | bytes 393220
  433.9 3.1 copy-start.8
Sparse Core Ops, SparseCore 0:
  124.6 42.8 all-reduce.4
  218.5 55.1 all-reduce.6
  279.2 154.6 all-reduce.8
